TPU v7x, 32 devices: a whole 2x2x4 slice. The times are simulated.
32 devices in a mesh: dap: 8 (over y, x, core), seq: 4 (over z).
Axes of the slice: x: 2, y: 2, z: 4, core: 2. Of those that a mesh axis runs over, the one named last changes fastest.
Arguments:
- homolog_tensor: bfloat16 [8, 32, 256], P('dap', 'seq'), may hold values from -6 to 6
- pair_features: bfloat16 [32, 32, 128], P('seq', 'dap'), may hold values from -6 to 6
- entry_real_mask: int32 [8, 32], P('dap', 'seq'), may hold values 0 or 1
- chain_ids: int32 [32], replicated, may hold values from 0 to 3, never falling along the last dimension, each value on 1 to 16 neighbouring positions
- horizontal_matrices: bfloat16 [256, 1024], replicated, may hold values from -0.375 to 0.375
- horizontal_projector: bfloat16 [256, 256], replicated, may hold values from -0.375 to 0.375
- bias_proj: float32 [128, 8], replicated, may hold values from -35.35534 to 35.35534
- chain_bias: float32 [2, 8], replicated, may hold values from -4 to 4
- column_proj: bfloat16 [256, 1024], replicated, may hold values from -12.5 to 12.5
- vertical_projector: bfloat16 [256, 256], replicated, may hold values from -0.375 to 0.375
- expansion_matrix: bfloat16 [256, 1024], replicated, may hold values from -0.375 to 0.375
- contraction_matrix: bfloat16 [1024, 256], replicated, may hold values from -0.1875 to 0.1875
Outputs:
- updated: bfloat16 [8, 32, 256], P('dap', 'seq')
Inputs may be any that keep to these rules, and one draw needn't show every extreme that they name: `chain_ids`: chain numbers never fall along the residues.
All inputs are finite; a program needn't handle non-finite values. No bound on the sum of `entry_real_mask` on one device may be relied on, other than what follows from the above.
Results may differ from a plain program's by a relative error of at most 0.013.
The roundings to bfloat16 on the way count: a program that leaves them out, or rounds other values in their place, can miss the bound.
Values may be sent and summed in bfloat16 or wider, within the bound.
No kernel may reach another device: no remote copies, remote signals or barrier semaphores. Data moves between devices by JAX's collectives and lax.ppermute only.
A program may use at most 64 MiB of HBM per device.

v0:
```python
import jax
import jax.numpy as jnp
from jax import lax
from jax.sharding import PartitionSpec as P

HEAD_TOTAL = 8
HEAD_DEPTH = 32
epsilon = 1e-05


def layer_norm(inputs):
    center = inputs - jnp.mean(inputs, axis=-1, keepdims=True)
    spread = jnp.mean(center * center, axis=-1, keepdims=True)
    return center * lax.rsqrt(spread + epsilon)


def attend(queries, key_part, value_part, keep_mask, bias_term):
    scores = jnp.einsum(
        "ihd,jhd->hij", queries, key_part, preferred_element_type=jnp.float32
    ) * HEAD_DEPTH ** (-0.5)
    if bias_term is not None:
        scores = scores + bias_term.astype(jnp.float32)
    scores = jnp.where(keep_mask[None, None, :] > 0, scores, -1000000000.0)
    weights = jax.nn.softmax(scores, axis=-1).astype(jnp.bfloat16)
    return jnp.einsum("hij,jhd->ihd", weights, value_part, preferred_element_type=jnp.float32)


def column_update(
    column, keep_column, column_proj, vertical_projector, expansion_matrix, contraction_matrix
):
    expanded_dimension = HEAD_TOTAL * HEAD_DEPTH
    standardized = layer_norm(column.astype(jnp.float32)).astype(jnp.bfloat16)
    projected = jnp.dot(standardized, column_proj, preferred_element_type=jnp.float32).astype(
        jnp.bfloat16
    )
    queries = projected[:, :expanded_dimension].reshape(-1, HEAD_TOTAL, HEAD_DEPTH)
    key_part = projected[:, expanded_dimension : 2 * expanded_dimension].reshape(
        -1, HEAD_TOTAL, HEAD_DEPTH
    )
    value_part = projected[:, 2 * expanded_dimension : 3 * expanded_dimension].reshape(
        -1, HEAD_TOTAL, HEAD_DEPTH
    )
    attended = attend(queries, key_part, value_part, keep_column, None).reshape(
        -1, expanded_dimension
    )
    sigmoid_scaled = (
        jax.nn.sigmoid(projected[:, 3 * expanded_dimension :].astype(jnp.float32)) * attended
    ).astype(jnp.bfloat16)
    mixed = column.astype(jnp.float32) + jnp.dot(
        sigmoid_scaled, vertical_projector, preferred_element_type=jnp.float32
    )
    inner = jnp.maximum(
        jnp.dot(
            layer_norm(mixed).astype(jnp.bfloat16),
            expansion_matrix,
            preferred_element_type=jnp.float32,
        ),
        0.0,
    ).astype(jnp.bfloat16)
    return (mixed + jnp.dot(inner, contraction_matrix, preferred_element_type=jnp.float32)).astype(
        jnp.bfloat16
    )


def body(
    homolog_tensor,
    pair_features,
    entry_real_mask,
    chain_ids,
    horizontal_matrices,
    horizontal_projector,
    bias_proj,
    chain_bias,
    column_proj,
    vertical_projector,
    expansion_matrix,
    contraction_matrix,
):
    row_count, local_residues, channels = homolog_tensor.shape
    expanded_dimension = HEAD_TOTAL * HEAD_DEPTH
    dap_count = lax.axis_size("dap")
    pair_rows, pair_columns, pair_width = pair_features.shape
    normed_pair = layer_norm(pair_features.astype(jnp.float32))
    projected_pair = jnp.einsum(
        "ijc,ch->hij", normed_pair, bias_proj, precision=lax.Precision.HIGHEST
    )
    row_chain = lax.dynamic_slice_in_dim(chain_ids, lax.axis_index("seq") * pair_rows, pair_rows)
    column_chain = lax.dynamic_slice_in_dim(
        chain_ids, lax.axis_index("dap") * pair_columns, pair_columns
    )
    same_chain = (row_chain[:, None] == column_chain[None, :]).astype(jnp.float32)
    chain_term = chain_bias[0][:, None, None] * same_chain + chain_bias[1][:, None, None] * (
        1.0 - same_chain
    )
    local_bias = (projected_pair + chain_term).astype(jnp.bfloat16)
    pair_bias = lax.all_gather(local_bias, "dap", axis=2, tiled=True)
    standardized = layer_norm(homolog_tensor.astype(jnp.float32)).astype(jnp.bfloat16)
    flat = standardized.reshape(-1, channels)
    keep_mask = entry_real_mask.astype(jnp.bfloat16)
    projected = (
        jnp.dot(flat, horizontal_matrices, preferred_element_type=jnp.float32)
        .astype(jnp.bfloat16)
        .reshape(row_count, local_residues, 4 * expanded_dimension)
    )
    queries = projected[..., :expanded_dimension]
    gating = projected[..., 3 * expanded_dimension :]
    key_values, keep_all = (
        lax.all_gather(
            projected[..., expanded_dimension : 3 * expanded_dimension], "seq", axis=1, tiled=True
        ),
        lax.all_gather(keep_mask, "seq", axis=1, tiled=True),
    )

    def one_row(inputs_row):
        row_queries, row_pairs, row_keep = inputs_row
        key_part = row_pairs[:, :expanded_dimension].reshape(-1, HEAD_TOTAL, HEAD_DEPTH)
        value_part = row_pairs[:, expanded_dimension:].reshape(-1, HEAD_TOTAL, HEAD_DEPTH)
        return attend(
            row_queries.reshape(local_residues, HEAD_TOTAL, HEAD_DEPTH),
            key_part,
            value_part,
            row_keep,
            pair_bias,
        ).reshape(local_residues, expanded_dimension)

    attended = lax.map(one_row, (queries, key_values, keep_all))
    sigmoid_scaled = (jax.nn.sigmoid(gating.astype(jnp.float32)) * attended).astype(jnp.bfloat16)
    row_result = jnp.dot(
        sigmoid_scaled.reshape(-1, expanded_dimension),
        horizontal_projector,
        preferred_element_type=jnp.float32,
    ).reshape(row_count, local_residues, channels)
    updated_rows = (homolog_tensor.astype(jnp.float32) + row_result).astype(jnp.bfloat16)
    per_device = local_residues // dap_count
    blocks = updated_rows.reshape(row_count, dap_count, per_device, channels)
    keep_blocks = keep_mask.reshape(row_count, dap_count, per_device)

    def single_column(inputs_col):
        return column_update(
            inputs_col[0],
            inputs_col[1],
            column_proj,
            vertical_projector,
            expansion_matrix,
            contraction_matrix,
        )

    column_block = lax.all_to_all(blocks, "dap", split_axis=1, concat_axis=0, tiled=True)
    column_keep = lax.all_to_all(keep_blocks, "dap", split_axis=1, concat_axis=0, tiled=True)
    inputs_col = (jnp.moveaxis(column_block[:, 0], 1, 0), jnp.moveaxis(column_keep[:, 0], 1, 0))
    output_list = lax.map(single_column, inputs_col)
    mixed = jnp.moveaxis(output_list, 0, 1)[:, None]
    returned = lax.all_to_all(mixed, "dap", split_axis=0, concat_axis=1, tiled=True)
    return returned.reshape(row_count, local_residues, channels)


def solution(mesh):
    placed = (
        P("dap", "seq", None),
        P("seq", "dap", None),
        P("dap", "seq"),
        P(),
        P(),
        P(),
        P(),
        P(),
        P(),
        P(),
        P(),
        P(),
    )
    return jax.shard_map(
        body, mesh=mesh, in_specs=placed, out_specs=P("dap", "seq", None), check_vma=False
    )
```

profile of v0, /device:TPU:0, one launch (start us, length us, event | category | flops | bytes accessed | tf_op | source)
XLA Modules:
  0.0 71.7 jit_solution(17577258312015481253)
XLA Ops:
  0.0 0.7 convert_bitcast_fusion.1
  0.7 0.7 copy.49
  1.4 5.2 %all-to-all-start.1 = ((bf16[1,8,1]{2,0,1:T(2,128)(2,1)}), bf16[1,8,1]{2,0,1:T(2,128)(2,1)S(1)}, u32[]{:S(2)}, u32[]{:S(2)}) async-start(bf16[1,8,1]{2,0,1:T(2,128)(2,1)} %copy.49), calls=%async_computation.1 | async-start | bytes 8192 | tf_op jit(solution)/shard_map/all_to_all | solution.py:149
  6.6 0.7 copy-done.12
  7.3 0.1 dynamic_slice.21
  7.3 0.1 dynamic_slice.20
  7.4 0.1 broadcast_subtract_fusion
  7.5 0.1 compare_convert_fusion
  7.6 0.5 copy-done.6
  8.0 0.1 convert_reduce_fusion.1
  8.1 0.2 fusion.38
  8.3 0.2 fusion.12
  8.6 0.6 copy-done.7
  9.2 0.7 copy-done.5
  9.9 0.1 convert_reduce_fusion
  10.0 0.2 fusion.24
  10.1 0.0 copy-start.9
  10.1 0.1 fusion.22
  10.2 0.6 copy-done.9
  10.8 0.7 copy-done.11
  11.5 0.1 fusion.13
  11.6 0.1 copy.43
  11.7 9.7 %all_gather.11 = bf16[8,8,32]{1,0,2:T(8,128)(2,1)S(1)} all-gather(bf16[8,8,4]{1,0,2:T(8,128)(2,1)S(1)} %copy.43), channel_id=1, replica_groups=mesh['dap'=8,'seq'=4] {'dap'}, dimensions={2}, use_global_device_ids=true | all-gather | bytes 4608 | tf_op jit(solution)/shard_map/all_gather | solution.py:96
  21.5 0.1 copy.44
  21.6 0.6 slice-done
  22.2 13.4 %all_gather.9 = bf16[1,32,512]{2,1,0:T(8,128)(2,1)S(1)} all-gather(bf16[1,8,512]{2,1,0:T(8,128)(2,1)S(1)} %slice-done), channel_id=1, replica_groups=mesh['dap'=8,'seq'=4] {'seq'}, dimensions={1}, use_global_device_ids=true | all-gather | bytes 40960 | tf_op jit(solution)/shard_map/all_gather | solution.py:108
  35.6 0.1 reshape.208
  35.7 0.6 slice-done.1
  36.2 0.1 reshape.207
  36.3 0.6 dynamic-slice
  37.6 0.2 dynamic-update-slice
  37.8 11.7 %all-reduce = bf16[32]{0:T(256)(128)(2,1)S(1)} all-reduce(bf16[32]{0:T(256)(128)(2,1)S(1)} %dynamic-update-slice), channel_id=1, replica_groups=mesh['dap'=8,'seq'=4] {'seq'}, use_global_device_ids=true, to_apply=%add | all-reduce | flops 32 | bytes 128
  49.5 0.1 fusion.8
  49.7 0.2 fusion.66
  49.9 0.1 reshape.206
  50.0 0.0 copy-start.3
  50.0 0.3 convolution_bitcast_fusion.1
  50.3 0.1 broadcast_in_dim.72
  50.3 0.5 copy-done.3
  50.9 0.1 copy-done.8
  51.0 0.1 fusion.19
  51.2 0.6 broadcast.220
  51.8 0.7 %reduce.5 = bf16[8,256]{1,0:T(8,128)(2,1)S(1)} reduce(bf16[8,1,1,256]{3,2,1,0:T(2,128)(2,1)S(1)} %bitcast.75, bf16[]{:T(256)} %broadcast.220), dimensions={1,2}, to_apply=%bitcast.73.reduce_sub_computation | reduce | bytes 8194
  52.5 0.6 reshape.228
  53.1 3.3 %all-to-all-start = ((bf16[8,2,128]{2,1,0:T(2,128)(2,1)}), bf16[8,2,128]{2,1,0:T(2,128)(2,1)S(1)}, u32[]{:S(2)}, u32[]{:S(2)}) async-start(bf16[8,2,128]{2,1,0:T(2,128)(2,1)} %reshape.228), calls=%async_computation | async-start | bytes 8192 | tf_op jit(solution)/shard_map/all_to_all | solution.py:148
  56.4 0.2 compare_reduce_fusion
  56.6 4.3 %all-to-all-done = bf16[8,2,128]{2,1,0:T(2,128)(2,1)S(1)} async-done(((bf16[8,2,128]{2,1,0:T(2,128)(2,1)}), bf16[8,2,128]{2,1,0:T(2,128)(2,1)S(1)}, u32[]{:S(2)}, u32[]{:S(2)}) %all-to-all-start) | async-done | bytes 4128 | tf_op jit(solution)/shard_map/all_to_all | solution.py:148
  61.0 0.1 convert_reduce_fusion.2
  61.1 0.2 fusion.40
  61.3 0.0 copy-start.4
  61.3 0.2 convolution_convert_fusion
  61.5 0.1 reshape.214
  61.6 0.1 reshape.215
  61.7 0.1 fusion.6
  61.8 0.2 fusion.67
  62.0 0.1 reshape.212
  62.1 0.2 convolution_bitcast_fusion
  62.3 0.1 reshape.216
  62.4 0.3 fusion.72
  62.7 0.2 multiply_reduce_fusion
  62.9 0.4 fusion.18
  63.3 0.7 reduce.6
  64.0 7.1 %all_to_all.12 = bf16[8,2,128]{2,1,0:T(2,128)(2,1)S(1)} all-to-all(bf16[8,2,128]{2,1,0:T(2,128)(2,1)S(1)} %reshape.230), channel_id=1, replica_groups=mesh['dap'=8,'seq'=4] {'dap'}, dimensions={0} | all-to-all | bytes 8192 | tf_op jit(solution)/shard_map/all_to_all | solution.py:153
  71.1 0.6 copy.83
  (39 shorter events, 0.2 us)
Async XLA Ops:
  0.0 8.3 %copy-start = (bf16[256,1024]{1,0:T(8,128)(2,1)S(1)}, bf16[256,1024]{1,0:T(8,128)(2,1)}, u32[]{:S(2)}) copy-start(bf16[256,1024]{1,0:T(8,128)(2,1)} %param.16) | copy-start | bytes 1572868
  1.4 51.7 %all-to-all-start.1 = ((bf16[1,8,1]{2,0,1:T(2,128)(2,1)}), bf16[1,8,1]{2,0,1:T(2,128)(2,1)S(1)}, u32[]{:S(2)}, u32[]{:S(2)}) async-start(bf16[1,8,1]{2,0,1:T(2,128)(2,1)} %copy.49), calls=%async_computation.1 | async-start | bytes 8192 | tf_op jit(solution)/shard_map/all_to_all | solution.py:149
  6.6 0.7 copy-start.12
  7.3 0.7 copy-start.6
  8.6 0.6 copy-start.7
  9.2 0.7 copy-start.5
  10.1 0.7 copy-start.9
  10.8 0.7 copy-start.11
  21.5 0.7 slice-start
  35.5 0.8 %copy-start.13 = (u32[32]{0:T(128)S(1)}, u32[32]{0:T(128)}, u32[]{:S(2)}) copy-start(u32[32]{0:T(128)} %constant.98) | copy-start | bytes 388
  35.5 0.7 slice-start.1
  35.5 25.7 %copy-start.10 = (bf16[256,1024]{1,0:T(8,128)(2,1)S(1)}, bf16[256,1024]{1,0:T(8,128)(2,1)}, u32[]{:S(2)}) copy-start(bf16[256,1024]{1,0:T(8,128)(2,1)} %param.20) | copy-start | bytes 1572868
  50.0 0.9 %copy-start.3 = (bf16[256,256]{1,0:T(8,128)(2,1)S(1)}, bf16[256,256]{1,0:T(8,128)(2,1)}, u32[]{:S(2)}) copy-start(bf16[256,256]{1,0:T(8,128)(2,1)} %param.17) | copy-start | bytes 393220
  50.3 0.7 %copy-start.8 = (bf16[1,8,1024]{2,1,0:T(8,128)(2,1)S(1)}, bf16[1,8,1024]{2,1,0:T(8,128)(2,1)}, u32[]{:S(2)}) copy-start(bf16[1,8,1024]{2,1,0:T(8,128)(2,1)} %copy-done.7) | copy-start | bytes 49156
  53.1 7.9 %all-to-all-start = ((bf16[8,2,128]{2,1,0:T(2,128)(2,1)}), bf16[8,2,128]{2,1,0:T(2,128)(2,1)S(1)}, u32[]{:S(2)}, u32[]{:S(2)}) async-start(bf16[8,2,128]{2,1,0:T(2,128)(2,1)} %reshape.228), calls=%async_computation | async-start | bytes 8192 | tf_op jit(solution)/shard_map/all_to_all | solution.py:148
  61.3 1.1 %copy-start.4 = (bf16[256,256]{1,0:T(8,128)(2,1)S(1)}, bf16[256,256]{1,0:T(8,128)(2,1)}, u32[]{:S(2)}) copy-start(bf16[256,256]{1,0:T(8,128)(2,1)} %param.21) | copy-start | bytes 393220
  61.3 1.6 %copy-start.2 = (bf16[256,1024]{1,0:T(8,128)(2,1)S(1)}, bf16[256,1024]{1,0:T(8,128)(2,1)}, u32[]{:S(2)}) copy-start(bf16[256,1024]{1,0:T(8,128)(2,1)} %param.22) | copy-start | bytes 1572868
  61.5 1.3 %copy-start.1 = (bf16[1024,256]{1,0:T(8,128)(2,1)S(1)}, bf16[1024,256]{1,0:T(8,128)(2,1)}, u32[]{:S(2)}) copy-start(bf16[1024,256]{1,0:T(8,128)(2,1)} %param.23) | copy-start | bytes 1572868
where the time goes:
time: 72.2 us; the launch traced here: 71.7 us
  blocking collectives  41.9 us (58%)
  local copies, waits for them, and re-layouts  9.98 us (14%)
  starting transfers between devices  8.51 us (12%)
  waiting for transfers between devices  4.3 us (6%)
  other arithmetic  3.88 us (5%)
  matrix products  2.23 us (3%)
  between operations  0.87 us (1%)
    all_gather x1, blocking collectives, body(): lax.all_gather(projected[..., expanded_dimension:3 * expanded_dimension],...  13.4 us
    unnamed x1, blocking collectives  11.7 us
    all_gather x1, blocking collectives, body(): pair_bias = lax.all_gather(local_bias, 'dap', axis=2, tiled=True)  9.75 us
    all_to_all x1, blocking collectives, body(): lax.all_to_all(mixed, 'dap', split_axis=0, concat_axis=1, tiled=True)  7.05 us
    unnamed x37, local copies, waits for them, and re-layouts  7.04 us
    all_to_all x1, starting transfers between devices, body(): lax.all_to_all(keep_blocks, 'dap', split_axis=1, concat_axis=0, tiled=True)  5.2 us
    all_to_all x1, waiting for transfers between devices, body(): lax.all_to_all(blocks, 'dap', split_axis=1, concat_axis=0, tiled=True)  4.3 us
    all_to_all x1, starting transfers between devices, body(): lax.all_to_all(blocks, 'dap', split_axis=1, concat_axis=0, tiled=True)  3.31 us
  transfers between devices with their start and end apart: 2, of which 1 were waited for; matrix products, arithmetic and copies ran while one was open for 8% of the time, Pallas kernels for 0%

commit v1 on v0

--- a/solution.py
+++ b/solution.py
@@ -6,6 +6,18 @@
 HEAD_TOTAL = 8
 HEAD_DEPTH = 32
 epsilon = 1e-05
+
+
+def split_up(value, dim, size):
+    lengths = value.shape
+    tiles = value.reshape(*lengths[:dim], size, lengths[dim] // size, *lengths[dim + 1 :])
+    return jnp.moveaxis(tiles, dim, 0)
+
+
+def in_order(pieces, dim):
+    pieces = jnp.moveaxis(pieces, 0, dim)
+    lengths = pieces.shape
+    return pieces.reshape(*lengths[:dim], lengths[dim] * lengths[dim + 1], *lengths[dim + 2 :])
 
 
 def layer_norm(inputs):
@@ -150,7 +162,15 @@
     inputs_col = (jnp.moveaxis(column_block[:, 0], 1, 0), jnp.moveaxis(column_keep[:, 0], 1, 0))
     output_list = lax.map(single_column, inputs_col)
     mixed = jnp.moveaxis(output_list, 0, 1)[:, None]
-    returned = lax.all_to_all(mixed, "dap", split_axis=0, concat_axis=1, tiled=True)
+    size, mine = (lax.axis_size("dap"), lax.axis_index("dap"))
+    blocks_2 = split_up(mixed, 0, size)
+    whole = blocks_2
+    for hop in range(1, size):
+        target, source = ((mine + hop) % size, (mine - hop) % size)
+        sent = lax.dynamic_index_in_dim(blocks_2, target, 0)
+        partner_block = lax.ppermute(sent, "dap", [(i, (i + hop) % size) for i in range(size)])
+        whole = lax.dynamic_update_slice_in_dim(whole, partner_block, source, axis=0)
+    returned = in_order(whole, 1)
     return returned.reshape(row_count, local_residues, channels)
 
 

time: 72.2 us -> 74 us (1.025)
  blocking collectives: 41.9 us -> 34.8 us
  starting transfers between devices: 8.51 us -> 15.5 us
  waiting for transfers between devices: 4.3 us -> 5.81 us
  local copies, waits for them, and re-layouts: 9.98 us -> 10.8 us
  other arithmetic: 3.88 us -> 3.13 us
    all_to_all x1 -> x0, blocking collectives: 7.05 us -> none  [body(): lax.all_to_all(mixed, 'dap', split_axis=0, concat_axis=1, tiled=True)]
    ppermute x0 -> x7, starting transfers between devices: none -> 6.99 us  [body(): lax.ppermute(sent, 'dap', [(i, (i + hop) % size) for i in range(size)])]
    ppermute x0 -> x7, waiting for transfers between devices: none -> 1.5 us  [body(): lax.ppermute(sent, 'dap', [(i, (i + hop) % size) for i in range(size)])]
    dynamic_update_slice x0 -> x7, local copies, waits for them, and re-layouts: none -> 1.5 us  [body(): lax.dynamic_update_slice_in_dim(whole, partner_block, source, axis=0)]
    unnamed x37 -> x36, local copies, waits for them, and re-layouts: 7.04 us -> 6.35 us
  transfers between devices with their start and end apart: 2 -> 9, of which waited for: 1 -> 3; matrix products, arithmetic and copies ran while one was open for 8% -> 8% of each run, Pallas kernels for 0% -> 0%
where the time goes in v1:
time: 74 us; the launch traced here: 73.2 us
  blocking collectives  34.8 us (47%)
  starting transfers between devices  15.5 us (21%)
  local copies, waits for them, and re-layouts  10.8 us (15%)
  waiting for transfers between devices  5.81 us (8%)
  other arithmetic  3.13 us (4%)
  matrix products  2.23 us (3%)
  between operations  0.92 us (1%)
    all_gather x1, blocking collectives, body(): lax.all_gather(projected[..., expanded_dimension:3 * expanded_dimension],...  13.4 us
    unnamed x1, blocking collectives  11.7 us
    all_gather x1, blocking collectives, body(): pair_bias = lax.all_gather(local_bias, 'dap', axis=2, tiled=True)  9.75 us
    ppermute x7, starting transfers between devices, body(): lax.ppermute(sent, 'dap', [(i, (i + hop) % size) for i in range(size)])  6.99 us
    unnamed x36, local copies, waits for them, and re-layouts  6.35 us
    all_to_all x1, starting transfers between devices, body(): lax.all_to_all(keep_blocks, 'dap', split_axis=1, concat_axis=0, tiled=True)  5.2 us
    all_to_all x1, waiting for transfers between devices, body(): lax.all_to_all(blocks, 'dap', split_axis=1, concat_axis=0, tiled=True)  4.3 us
    all_to_all x1, starting transfers between devices, body(): lax.all_to_all(blocks, 'dap', split_axis=1, concat_axis=0, tiled=True)  3.31 us
  transfers between devices with their start and end apart: 9, of which 3 were waited for; matrix products, arithmetic and copies ran while one was open for 8% of the time, Pallas kernels for 0%

profile of v1, /device:TPU:0, one launch (start us, length us, event | category | flops | bytes accessed | tf_op | source)
XLA Modules:
  0.0 73.2 jit_solution(17179305332908810068)
XLA Ops:
  0.0 0.7 convert_bitcast_fusion.1
  0.7 0.7 copy.48
  1.4 5.2 %all-to-all-start.1 = ((bf16[1,8,1]{2,0,1:T(2,128)(2,1)}), bf16[1,8,1]{2,0,1:T(2,128)(2,1)S(1)}, u32[]{:S(2)}, u32[]{:S(2)}) async-start(bf16[1,8,1]{2,0,1:T(2,128)(2,1)} %copy.48), calls=%async_computation.1 | async-start | bytes 8192 | tf_op jit(solution)/shard_map/all_to_all | solution.py:161
  6.6 0.7 copy-done.13
  7.3 0.1 dynamic_slice.57
  7.4 0.1 broadcast_subtract_fusion
  7.6 0.5 copy-done.6
  8.0 0.1 convert_reduce_fusion.1
  8.1 0.2 fusion.37
  8.3 0.2 fusion.12
  8.6 0.6 copy-done.7
  9.2 0.7 copy-done.5
  9.9 0.1 convert_reduce_fusion
  10.0 0.2 fusion.23
  10.1 0.1 fusion.21
  10.2 0.6 copy-done.10
  10.8 0.7 copy-done.12
  11.5 0.1 fusion.13
  11.6 0.1 copy.42
  11.7 9.7 %all_gather.11 = bf16[8,8,32]{1,0,2:T(8,128)(2,1)S(1)} all-gather(bf16[8,8,4]{1,0,2:T(8,128)(2,1)S(1)} %copy.42), channel_id=1, replica_groups=mesh['dap'=8,'seq'=4] {'dap'}, dimensions={2}, use_global_device_ids=true | all-gather | bytes 4608 | tf_op jit(solution)/shard_map/all_gather | solution.py:108
  21.5 0.1 copy.43
  21.6 0.6 slice-done
  22.2 13.4 %all_gather.9 = bf16[1,32,512]{2,1,0:T(8,128)(2,1)S(1)} all-gather(bf16[1,8,512]{2,1,0:T(8,128)(2,1)S(1)} %slice-done), channel_id=1, replica_groups=mesh['dap'=8,'seq'=4] {'seq'}, dimensions={1}, use_global_device_ids=true | all-gather | bytes 40960 | tf_op jit(solution)/shard_map/all_gather | solution.py:120
  35.6 0.1 reshape.223
  35.7 0.6 slice-done.1
  36.2 0.1 reshape.222
  36.3 0.6 dynamic-slice.7
  37.6 0.2 dynamic-update-slice
  37.8 11.7 %all-reduce = bf16[32]{0:T(256)(128)(2,1)S(1)} all-reduce(bf16[32]{0:T(256)(128)(2,1)S(1)} %dynamic-update-slice), channel_id=1, replica_groups=mesh['dap'=8,'seq'=4] {'seq'}, use_global_device_ids=true, to_apply=%add | all-reduce | flops 32 | bytes 128
  49.5 0.1 fusion.8
  49.7 0.2 fusion.72
  49.9 0.1 reshape.221
  50.0 0.3 convolution_bitcast_fusion.1
  50.3 0.1 broadcast_in_dim.72
  50.3 0.5 copy-done.3
  50.9 0.1 copy-done.8
  51.0 0.1 fusion.18
  51.2 0.5 broadcast.234
  51.7 0.7 reduce.5
  52.3 0.6 reshape.242
  53.0 3.3 %all-to-all-start = ((bf16[8,2,128]{2,1,0:T(2,128)(2,1)}), bf16[8,2,128]{2,1,0:T(2,128)(2,1)S(1)}, u32[]{:S(2)}, u32[]{:S(2)}) async-start(bf16[8,2,128]{2,1,0:T(2,128)(2,1)} %reshape.242), calls=%async_computation | async-start | bytes 8192 | tf_op jit(solution)/shard_map/all_to_all | solution.py:160
  56.3 0.2 compare_reduce_fusion
  56.5 4.3 %all-to-all-done = bf16[8,2,128]{2,1,0:T(2,128)(2,1)S(1)} async-done(((bf16[8,2,128]{2,1,0:T(2,128)(2,1)}), bf16[8,2,128]{2,1,0:T(2,128)(2,1)S(1)}, u32[]{:S(2)}, u32[]{:S(2)}) %all-to-all-start) | async-done | bytes 4128 | tf_op jit(solution)/shard_map/all_to_all | solution.py:160
  60.8 0.1 convert_reduce_fusion.2
  61.0 0.2 fusion.39
  61.2 0.2 convolution_convert_fusion
  61.4 0.1 reshape.229
  61.5 0.1 reshape.230
  61.6 0.1 fusion.6
  61.7 0.2 fusion.73
  61.9 0.1 reshape.227
  62.0 0.2 convolution_bitcast_fusion
  62.2 0.1 reshape.231
  62.3 0.3 fusion.78
  62.5 0.2 multiply_reduce_fusion
  62.7 0.4 fusion.17
  63.3 0.6 collective-permute-start.1
  63.9 1.4 %collective-permute-start.2 = (bf16[1,1,1,1,256]{4,3,2,1,0:T(2,128)(2,1)S(1)}, bf16[1,1,1,1,256]{4,3,2,1,0:T(2,128)(2,1)S(1)}, u32[]{:S(2)}, u32[]{:S(2)}) collective-permute-start(bf16[1,1,1,1,256]{4,3,2,1,0:T(2,128)(2,1)S(1)} %get-tuple-element.56), channel_id=1, source_target_pairs={{0,12},{4,16},{8,20},{12,24},{16,28},{20,0},{24,4},{28,8},{1,13},{... | collective-permute-start | bytes 1544 | tf_op jit(solution)/shard_map/ppermute | solution.py:171
  65.2 1.5 %collective-permute-start.3 = (bf16[1,1,1,1,256]{4,3,2,1,0:T(2,128)(2,1)S(1)}, bf16[1,1,1,1,256]{4,3,2,1,0:T(2,128)(2,1)S(1)}, u32[]{:S(2)}, u32[]{:S(2)}) collective-permute-start(bf16[1,1,1,1,256]{4,3,2,1,0:T(2,128)(2,1)S(1)} %get-tuple-element.47), channel_id=1, source_target_pairs={{0,16},{4,20},{8,24},{12,28},{16,0},{20,4},{24,8},{28,12},{1,17},{... | collective-permute-start | bytes 1544 | tf_op jit(solution)/shard_map/ppermute | solution.py:171
  66.7 0.4 collective-permute-done
  67.1 2.0 %collective-permute-start.5 = (bf16[1,1,1,1,256]{4,3,2,1,0:T(2,128)(2,1)S(1)}, bf16[1,1,1,1,256]{4,3,2,1,0:T(2,128)(2,1)S(1)}, u32[]{:S(2)}, u32[]{:S(2)}) collective-permute-start(bf16[1,1,1,1,256]{4,3,2,1,0:T(2,128)(2,1)S(1)} %get-tuple-element.45), channel_id=1, source_target_pairs={{0,24},{4,28},{8,0},{12,4},{16,8},{20,12},{24,16},{28,20},{1,25},{... | collective-permute-start | bytes 1544 | tf_op jit(solution)/shard_map/ppermute | solution.py:171
  69.1 1.5 %collective-permute-start.6 = (bf16[1,1,1,1,256]{4,3,2,1,0:T(2,128)(2,1)S(1)}, bf16[1,1,1,1,256]{4,3,2,1,0:T(2,128)(2,1)S(1)}, u32[]{:S(2)}, u32[]{:S(2)}) collective-permute-start(bf16[1,1,1,1,256]{4,3,2,1,0:T(2,128)(2,1)S(1)} %get-tuple-element.44), channel_id=1, source_target_pairs={{0,28},{4,0},{8,4},{12,8},{16,12},{20,16},{24,20},{28,24},{1,29},{... | collective-permute-start | bytes 1544 | tf_op jit(solution)/shard_map/ppermute | solution.py:171
  70.8 1.1 %collective-permute-done.6 = bf16[1,1,1,1,256]{4,3,2,1,0:T(2,128)(2,1)S(1)} collective-permute-done((bf16[1,1,1,1,256]{4,3,2,1,0:T(2,128)(2,1)S(1)}, bf16[1,1,1,1,256]{4,3,2,1,0:T(2,128)(2,1)S(1)}, u32[]{:S(2)}, u32[]{:S(2)}) %collective-permute-start.6) | collective-permute-done | bytes 544 | tf_op jit(solution)/shard_map/ppermute | solution.py:171
  71.9 1.3 %dynamic_update_slice.40 = bf16[1,8,256]{2,1,0:T(8,128)(2,1)} dynamic-update-slice(bf16[1,8,256]{2,1,0:T(8,128)(2,1)} %copy-done.9, bf16[1,1,256]{2,1,0:T(2,128)(2,1)S(1)} %bitcast.98, s32[]{:T(128)} %constant.190.clone.1, s32[]{:T(128)S(6)} %select_n.149, s32[]{:T(128)} %constant.190.clone.1) | dynamic-update-slice | bytes 1028 | tf_op jit(solution)/shard_map/dynamic_update_slice | solution.py:172
  (58 shorter events, 0.6 us)
Async XLA Ops:
  0.0 8.3 %copy-start = (bf16[256,1024]{1,0:T(8,128)(2,1)S(1)}, bf16[256,1024]{1,0:T(8,128)(2,1)}, u32[]{:S(2)}) copy-start(bf16[256,1024]{1,0:T(8,128)(2,1)} %param.16) | copy-start | bytes 1572868
  1.4 51.5 %all-to-all-start.1 = ((bf16[1,8,1]{2,0,1:T(2,128)(2,1)}), bf16[1,8,1]{2,0,1:T(2,128)(2,1)S(1)}, u32[]{:S(2)}, u32[]{:S(2)}) async-start(bf16[1,8,1]{2,0,1:T(2,128)(2,1)} %copy.48), calls=%async_computation.1 | async-start | bytes 8192 | tf_op jit(solution)/shard_map/all_to_all | solution.py:161
  6.6 0.7 copy-start.13
  7.3 0.7 copy-start.6
  8.6 0.6 copy-start.7
  9.2 0.7 copy-start.5
  10.1 0.7 copy-start.10
  10.8 0.7 copy-start.12
  21.5 0.7 slice-start
  35.5 0.8 %copy-start.14 = (u32[32]{0:T(128)S(1)}, u32[32]{0:T(128)}, u32[]{:S(2)}) copy-start(u32[32]{0:T(128)} %constant.215) | copy-start | bytes 388
  35.5 0.7 slice-start.1
  35.5 25.6 %copy-start.11 = (bf16[256,1024]{1,0:T(8,128)(2,1)S(1)}, bf16[256,1024]{1,0:T(8,128)(2,1)}, u32[]{:S(2)}) copy-start(bf16[256,1024]{1,0:T(8,128)(2,1)} %param.20) | copy-start | bytes 1572868
  50.0 0.9 %copy-start.3 = (bf16[256,256]{1,0:T(8,128)(2,1)S(1)}, bf16[256,256]{1,0:T(8,128)(2,1)}, u32[]{:S(2)}) copy-start(bf16[256,256]{1,0:T(8,128)(2,1)} %param.17) | copy-start | bytes 393220
  50.3 0.7 %copy-start.8 = (bf16[1,8,1024]{2,1,0:T(8,128)(2,1)S(1)}, bf16[1,8,1024]{2,1,0:T(8,128)(2,1)}, u32[]{:S(2)}) copy-start(bf16[1,8,1024]{2,1,0:T(8,128)(2,1)} %copy-done.7) | copy-start | bytes 49156
  53.0 7.9 %all-to-all-start = ((bf16[8,2,128]{2,1,0:T(2,128)(2,1)}), bf16[8,2,128]{2,1,0:T(2,128)(2,1)S(1)}, u32[]{:S(2)}, u32[]{:S(2)}) async-start(bf16[8,2,128]{2,1,0:T(2,128)(2,1)} %reshape.242), calls=%async_computation | async-start | bytes 8192 | tf_op jit(solution)/shard_map/all_to_all | solution.py:160
  61.2 1.1 %copy-start.4 = (bf16[256,256]{1,0:T(8,128)(2,1)S(1)}, bf16[256,256]{1,0:T(8,128)(2,1)}, u32[]{:S(2)}) copy-start(bf16[256,256]{1,0:T(8,128)(2,1)} %param.21) | copy-start | bytes 393220
  61.2 1.6 %copy-start.2 = (bf16[256,1024]{1,0:T(8,128)(2,1)S(1)}, bf16[256,1024]{1,0:T(8,128)(2,1)}, u32[]{:S(2)}) copy-start(bf16[256,1024]{1,0:T(8,128)(2,1)} %param.22) | copy-start | bytes 1572868
  61.4 1.3 %copy-start.1 = (bf16[1024,256]{1,0:T(8,128)(2,1)S(1)}, bf16[1024,256]{1,0:T(8,128)(2,1)}, u32[]{:S(2)}) copy-start(bf16[1024,256]{1,0:T(8,128)(2,1)} %param.23) | copy-start | bytes 1572868
  63.2 4.0 %collective-permute-start = (bf16[1,1,1,1,256]{4,3,2,1,0:T(2,128)(2,1)S(1)}, bf16[1,1,1,1,256]{4,3,2,1,0:T(2,128)(2,1)S(1)}, u32[]{:S(2)}, u32[]{:S(2)}) collective-permute-start(bf16[1,1,1,1,256]{4,3,2,1,0:T(2,128)(2,1)S(1)} %get-tuple-element.60), channel_id=1, source_target_pairs={{0,4},{4,8},{8,12},{12,16},{16,20},{20,24},{24,28},{28,0},{1,5},{5... | collective-permute-start | bytes 1544 | tf_op jit(solution)/shard_map/ppermute | solution.py:171
  63.3 5.9 %collective-permute-start.1 = (bf16[1,1,1,1,256]{4,3,2,1,0:T(2,128)(2,1)S(1)}, bf16[1,1,1,1,256]{4,3,2,1,0:T(2,128)(2,1)S(1)}, u32[]{:S(2)}, u32[]{:S(2)}) collective-permute-start(bf16[1,1,1,1,256]{4,3,2,1,0:T(2,128)(2,1)S(1)} %get-tuple-element.58), channel_id=1, source_target_pairs={{0,8},{4,12},{8,16},{12,20},{16,24},{20,28},{24,0},{28,4},{1,9},{5... | collective-permute-start | bytes 1544 | tf_op jit(solution)/shard_map/ppermute | solution.py:171
  63.9 6.8 %collective-permute-start.2 = (bf16[1,1,1,1,256]{4,3,2,1,0:T(2,128)(2,1)S(1)}, bf16[1,1,1,1,256]{4,3,2,1,0:T(2,128)(2,1)S(1)}, u32[]{:S(2)}, u32[]{:S(2)}) collective-permute-start(bf16[1,1,1,1,256]{4,3,2,1,0:T(2,128)(2,1)S(1)} %get-tuple-element.56), channel_id=1, source_target_pairs={{0,12},{4,16},{8,20},{12,24},{16,28},{20,0},{24,4},{28,8},{1,13},{... | collective-permute-start | bytes 1544 | tf_op jit(solution)/shard_map/ppermute | solution.py:171
  65.2 5.5 %collective-permute-start.3 = (bf16[1,1,1,1,256]{4,3,2,1,0:T(2,128)(2,1)S(1)}, bf16[1,1,1,1,256]{4,3,2,1,0:T(2,128)(2,1)S(1)}, u32[]{:S(2)}, u32[]{:S(2)}) collective-permute-start(bf16[1,1,1,1,256]{4,3,2,1,0:T(2,128)(2,1)S(1)} %get-tuple-element.47), channel_id=1, source_target_pairs={{0,16},{4,20},{8,24},{12,28},{16,0},{20,4},{24,8},{28,12},{1,17},{... | collective-permute-start | bytes 1544 | tf_op jit(solution)/shard_map/ppermute | solution.py:171
  66.7 4.0 %collective-permute-start.4 = (bf16[1,1,1,1,256]{4,3,2,1,0:T(2,128)(2,1)S(1)}, bf16[1,1,1,1,256]{4,3,2,1,0:T(2,128)(2,1)S(1)}, u32[]{:S(2)}, u32[]{:S(2)}) collective-permute-start(bf16[1,1,1,1,256]{4,3,2,1,0:T(2,128)(2,1)S(1)} %get-tuple-element.46), channel_id=1, source_target_pairs={{0,20},{4,24},{8,28},{12,0},{16,4},{20,8},{24,12},{28,16},{1,21},{... | collective-permute-start | bytes 1544 | tf_op jit(solution)/shard_map/ppermute | solution.py:171
  67.1 3.7 %collective-permute-start.5 = (bf16[1,1,1,1,256]{4,3,2,1,0:T(2,128)(2,1)S(1)}, bf16[1,1,1,1,256]{4,3,2,1,0:T(2,128)(2,1)S(1)}, u32[]{:S(2)}, u32[]{:S(2)}) collective-permute-start(bf16[1,1,1,1,256]{4,3,2,1,0:T(2,128)(2,1)S(1)} %get-tuple-element.45), channel_id=1, source_target_pairs={{0,24},{4,28},{8,0},{12,4},{16,8},{20,12},{24,16},{28,20},{1,25},{... | collective-permute-start | bytes 1544 | tf_op jit(solution)/shard_map/ppermute | solution.py:171
  69.1 2.8 %collective-permute-start.6 = (bf16[1,1,1,1,256]{4,3,2,1,0:T(2,128)(2,1)S(1)}, bf16[1,1,1,1,256]{4,3,2,1,0:T(2,128)(2,1)S(1)}, u32[]{:S(2)}, u32[]{:S(2)}) collective-permute-start(bf16[1,1,1,1,256]{4,3,2,1,0:T(2,128)(2,1)S(1)} %get-tuple-element.44), channel_id=1, source_target_pairs={{0,28},{4,0},{8,4},{12,8},{16,12},{20,16},{24,20},{28,24},{1,29},{... | collective-permute-start | bytes 1544 | tf_op jit(solution)/shard_map/ppermute | solution.py:171
  70.8 1.1 %copy-start.9 = (bf16[1,8,256]{2,1,0:T(8,128)(2,1)}, bf16[1,8,256]{2,1,0:T(8,128)(2,1)S(1)}, u32[]{:S(2)}) copy-start(bf16[1,8,256]{2,1,0:T(8,128)(2,1)S(1)} %dynamic_update_slice.39) | copy-start | bytes 12292
